TPU v7x, 128 devices: a whole 4x4x4 slice. The times are simulated.
128 devices in a mesh: store: 8 (over z_lo, y), mod: 16 (over z_hi, x, core).
Axes of the slice: x: 4, y: 4, z: 4 (z_hi: 2, z_lo: 2; z = z_hi * 2 + z_lo), core: 2. Of those that a mesh axis runs over, the one named last changes fastest.
Arguments:
- act_proj: bfloat16 [1024, 256, 1024], P(('store', 'mod')), may hold values from -1.5 to 1.5
- grad_proj: bfloat16 [1024, 256, 1024], P(('store', 'mod')), may hold values from -1.5 to 1.5
- token_mask: int32 [1024, 256], P(('store', 'mod')), may hold values 0 or 1
- layer_of: int32 [32], P('mod'), may hold values from 0 to 3, as said below
- layer_weight: float32 [4], replicated, may hold values from 0.25 to 4
- fisher_inv: bfloat16 [32, 1024, 1024], P('mod'), may hold values from -0.2 to 1.8
- stored_grads: bfloat16 [32768, 32768], P('store', 'mod'), may hold values from -0.049804688 to 0.049804688
Outputs:
- scores: float32 [1024, 32768], P('mod', 'store')
Inputs may be any that keep to these rules, and one draw needn't show every extreme that they name: `layer_of`: each of the 4 layers holds the same number of modules.
All inputs are finite; a program needn't handle non-finite values. No bound on the sum of `token_mask` on one device may be relied on, other than what follows from the above.
Results may differ from a plain program's by a relative error of at most 0.004.
Values may be sent and summed in bfloat16 or wider, within the bound.
No kernel may reach another device: no remote copies, remote signals or barrier semaphores. Data moves between devices by JAX's collectives and lax.ppermute only.
A program may use at most 128 MiB of HBM per device.

v0:
```python
import jax
import jax.numpy as jnp
from jax import lax
from jax.experimental import pallas as pl
from jax.experimental.pallas import tpu as pltpu
from jax.sharding import PartitionSpec as P

R = 32


def mod_perm(dz, dx, dc):
    pairs = []
    for m in range(16):
        z, x, c = m // 8, m // 2 % 4, m % 2
        pairs.append((m, (z + dz) % 2 * 8 + (x + dx) % 4 * 2 + (c + dc) % 2))
    return pairs


def store_perm(dz, dy):
    return [(s, (s // 4 + dz) % 2 * 4 + (s % 4 + dy) % 4) for s in range(8)]


def over_x(v, step):
    return lax.ppermute(v, "mod", mod_perm(0, step, 0))


def over_z_hi(v):
    return lax.ppermute(v, "mod", mod_perm(1, 0, 0))


def over_core(v):
    return lax.ppermute(v, "mod", mod_perm(0, 0, 1))


def over_y(v, step):
    return lax.ppermute(v, "store", store_perm(0, step))


def over_z_lo(v):
    return lax.ppermute(v, "store", store_perm(1, 0))


def pick(v, index, axis):
    return lax.dynamic_index_in_dim(v, index, axis, keepdims=False)


def gather_z_first(block):
    pair = jnp.stack([block, over_z_lo(block)])
    left = over_y(pair, 1)
    right = over_y(pair, -1)
    far = jnp.stack([over_y(left[0], 1), over_y(right[1], -1)])
    return jnp.stack([pair, left, far, right]).reshape(-1, block.shape[-1])


def gather_y_first(block):
    half = block.shape[0] // 2
    left = over_y(block, 1)
    right = over_y(block, -1)
    near = over_z_lo(jnp.stack([block, left, right]))
    far = jnp.concatenate([over_y(left[:half], 1), over_y(right[half:], -1)])
    far_z = over_z_lo(far)
    rows = [block, near[0], left, near[1], far, far_z, right, near[2]]
    return jnp.stack(rows).reshape(-1, block.shape[-1])


def add(*terms):
    total = terms[0].astype(jnp.float32)
    for term in terms[1:]:
        total = total + term.astype(jnp.float32)
    return total


def reduce_x(blocks, y, x):
    def block(step):
        return pick(blocks, (y - x - step) % 4, 0)

    half = blocks.shape[1] // 2
    to_next, to_prev, to_far, mine = block(1), block(-1), block(2), block(0)
    from_prev = over_x(jnp.stack([to_next[half:], to_far[:half]]), 1)
    from_next = over_x(jnp.stack([to_prev[:half], to_far[half:]]), -1)
    sum_prev = over_x(add(to_next[:half], from_prev[1]).astype(jnp.bfloat16), 1)
    sum_next = over_x(add(to_prev[half:], from_next[1]).astype(jnp.bfloat16), -1)
    low = add(mine[:half], from_next[0], sum_prev)
    high = add(mine[half:], from_prev[0], sum_next)
    return jnp.concatenate([low, high])


def scatter_x_first(part, y, x, z_mine):
    rows, width = part.shape[2], part.shape[3]
    reduced = reduce_x(part.reshape(4, 2 * rows, width), y, x).reshape(2, rows, width)
    received = over_z_hi(pick(reduced, 1 - z_mine, 0).astype(jnp.bfloat16))
    return add(pick(reduced, z_mine, 0), received)


def scatter_z_first(part, y, x, z_mine):
    received = over_z_hi(pick(part, 1 - z_mine, 1))
    both = add(pick(part, z_mine, 1), received).astype(jnp.bfloat16)
    return reduce_x(both, y, x)


STEP = 4


def outer_kernel(mask_ref, grad_ref, act_ref, out_ref, diag_ref):
    module = lax.broadcasted_iota(jnp.int32, (R, 256), 1) // R
    slot = lax.broadcasted_iota(jnp.int32, (8, 128), 1) // R
    for q in range(STEP):
        mask = mask_ref[pl.ds(pl.program_id(0) * STEP + q, 1), :].astype(jnp.bfloat16)
        for group in range(4):
            columns = slice(group * 256, group * 256 + 256)
            grad_side = grad_ref[q, :, columns].T * mask
            full = jnp.dot(grad_side, act_ref[q, :, columns], preferred_element_type=jnp.float32)
            diag = full[:R]
            for m in range(1, 8):
                diag = jnp.where(module == m, full[m * R : m * R + R], diag)
            for tile in range(2):
                start = (q * 8 + 2 * group + tile) * R
                diag_ref[start : start + R, :] = diag[:, tile * 128 : tile * 128 + 128]
        for tile in range(8):
            start = (q * 8 + tile) * R
            rows = [diag_ref[pl.ds(start + p, 8, stride=4), :] for p in range(4)]
            packed = []
            for a in range(4):
                merged = None
                for p in range(4):
                    moved = rows[p] if p == a else pltpu.roll(rows[p], (p - a) % 4 * R, 1)
                    merged = moved if p == 0 else jnp.where(slot == p, moved, merged)
                packed.append(merged)
            for k in range(2):
                pair = jnp.concatenate(packed[2 * k : 2 * k + 2], axis=0)
                out_ref[2 * tile + k, q] = pair.astype(jnp.bfloat16)


def outer_products(token_mask, grad_proj, act_proj):
    queries, length, columns = grad_proj.shape
    return pl.pallas_call(
        outer_kernel,
        grid=(queries // STEP,),
        in_specs=[
            pl.BlockSpec((queries, length), lambda q: (0, 0)),
            pl.BlockSpec((STEP, length, columns), lambda q: (q, 0, 0)),
            pl.BlockSpec((STEP, length, columns), lambda q: (q, 0, 0)),
        ],
        out_specs=pl.BlockSpec((16, STEP, 16, 128), lambda q: (0, q, 0, 0)),
        out_shape=jax.ShapeDtypeStruct((16, queries, 16, 128), jnp.bfloat16),
        scratch_shapes=[pltpu.VMEM((STEP * 8 * R, 128), jnp.float32)],
    )(token_mask, grad_proj, act_proj)


def fisher_kernel(core_ref, weight_ref, rows_ref, fisher_ref, sibling_ref, own_ref, wide_ref):
    module = pl.program_id(0)

    @pl.when(module == 0)
    def _():
        wide_ref[...] = rows_ref[...].reshape(wide_ref.shape).astype(jnp.float32)

    count = wide_ref.shape[0] // 16
    pieces = [wide_ref[pl.ds(module * 8 + r, count, stride=16), :] for r in range(8)]
    left = jnp.concatenate(pieces, axis=1).astype(jnp.bfloat16)
    product = jnp.dot(left, fisher_ref[0], preferred_element_type=jnp.float32)
    scaled = (product * weight_ref[module]).astype(jnp.bfloat16)
    first = core_ref[0] == 0
    half = count // 2

    @pl.when(first)
    def _():
        own_ref[...] = scaled[:half]
        sibling_ref[...] = scaled[half:]

    @pl.when(jnp.logical_not(first))
    def _():
        own_ref[...] = scaled[half:]
        sibling_ref[...] = scaled[:half]


def conditioned_rows(core, module_weight, grouped, fisher_inv):
    sources, queries = grouped.shape[:2]
    modules, rank = fisher_inv.shape[:2]
    count = sources * queries
    out = jax.ShapeDtypeStruct((count // 2, modules * rank), jnp.bfloat16)
    out_spec = pl.BlockSpec((count // 2, rank), lambda m: (0, m))
    return pl.pallas_call(
        fisher_kernel,
        grid=(modules,),
        in_specs=[
            pl.BlockSpec(memory_space=pltpu.SMEM),
            pl.BlockSpec(memory_space=pltpu.SMEM),
            pl.BlockSpec(memory_space=pltpu.VMEM),
            pl.BlockSpec((1, rank, rank), lambda m: (m, 0, 0)),
        ],
        out_specs=[out_spec, out_spec],
        out_shape=[out, out],
        scratch_shapes=[pltpu.VMEM((count * 16, 128), jnp.float32)],
    )(core[None], module_weight, grouped, fisher_inv)


def compute(act_proj, grad_proj, token_mask, layer_of, layer_weight, fisher_inv, stored_grads):
    place = lax.axis_index("mod")
    z_hi, x, core = place // 8, place // 2 % 4, place % 2
    owner = lax.axis_index("store")
    z_lo, y = owner // 4, owner % 4
    z_mine = (z_lo + z_hi) % 2
    per_sample = outer_products(token_mask, grad_proj, act_proj)
    picked = layer_of[:, None] == jnp.arange(layer_weight.shape[0], dtype=jnp.int32)[None, :]
    module_weight = jnp.sum(jnp.where(picked, layer_weight[None, :], 0.0), axis=1)
    grouped = lax.all_to_all(per_sample, "mod", split_axis=0, concat_axis=0, tiled=True)
    sibling, mine = conditioned_rows(core, module_weight, grouped, fisher_inv)
    half = mine.shape[0]
    sibling_rows = gather_z_first(sibling)
    own_rows = gather_y_first(mine)
    dims = (((1,), (1,)), ((), ()))
    cut = stored_grads.shape[0] * 3 // 8
    stored = [stored_grads[:cut], stored_grads[cut:]]
    swapped = []
    for n in range(2):
        partial = lax.dot_general(sibling_rows, stored[n], dims, preferred_element_type=jnp.float32)
        partial = partial.astype(jnp.bfloat16)
        swapped.append(over_core(partial))
    outs = []
    for n, scatter in ((0, scatter_z_first), (1, scatter_x_first)):
        own = lax.dot_general(own_rows, stored[n], dims, preferred_element_type=jnp.float32)
        part = add(own, swapped[n]).astype(jnp.bfloat16).reshape(4, 2, half, -1)
        outs.append(scatter(part, y, x, z_mine))
    return jnp.concatenate(outs, axis=1)


def solution(mesh):
    in_specs = (
        P(("store", "mod"), None, None),
        P(("store", "mod"), None, None),
        P(("store", "mod"), None),
        P("mod"),
        P(),
        P("mod", None, None),
        P("store", "mod"),
    )
    out_specs = P("mod", "store")
    return jax.shard_map(compute, mesh=mesh, in_specs=in_specs, out_specs=out_specs, check_vma=False)
```

profile of v0, /device:TPU:0, one launch (start us, length us, event | category | flops | bytes accessed | tf_op | source)
XLA Modules:
  0.0 154.0 jit_solution(18263562025445939546)
XLA Ops:
  0.0 5.1 %shard_map.73 = bf16[16,8,16,128]{3,2,1,0:T(8,128)(2,1)} custom-call(s32[8,256]{1,0:T(8,128)} %mask_ref.1, bf16[8,256,1024]{2,1,0:T(8,128)(2,1)} %grad_ref.1, bf16[8,256,1024]{2,1,0:T(8,128)(2,1)} %act_ref.1), custom_call_target="tpu_custom_call" | custom-call | tf_op jit(solution)/shard_map/pallas_call | solution.py:136
  5.1 7.8 %all-to-all-start = ((bf16[16,8,16,128]{3,2,1,0:T(8,128)(2,1)}), bf16[16,8,16,128]{3,2,1,0:T(8,128)(2,1)S(1)}, u32[]{:S(2)}, u32[]{:S(2)}) async-start(bf16[16,8,16,128]{3,2,1,0:T(8,128)(2,1)} %shard_map.73), calls=%async_computation | async-start | bytes 1048576 | tf_op jit(solution)/shard_map/all_to_all | solution.py:206
  13.0 0.7 fusion.28.weight_ref
  13.7 11.6 %all-to-all-done.rows_ref = bf16[16,8,16,128]{3,2,1,0:T(8,128)(2,1)S(1)} async-done(((bf16[16,8,16,128]{3,2,1,0:T(8,128)(2,1)}), bf16[16,8,16,128]{3,2,1,0:T(8,128)(2,1)S(1)}, u32[]{:S(2)}, u32[]{:S(2)}) %all-to-all-start) | async-done | bytes 524320 | tf_op jit(solution)/shard_map/all_to_all | solution.py:206
  25.3 0.8 copy-done
  26.1 3.7 %shard_map.74 = (bf16[64,2048]{1,0:T(8,128)(2,1)}, bf16[64,2048]{1,0:T(8,128)(2,1)}) custom-call(s32[1]{0:T(128)} %bitcast.core_ref, f32[2]{0:T(128)} %fusion.28.weight_ref, bf16[16,8,16,128]{3,2,1,0:T(8,128)(2,1)} %copy-done, bf16[2,1024,1024]{2,1,0:T(8,128)(2,1)} %fisher_ref.1), custom_call_target="tpu_custom_call" | custom-call | tf_op jit(solution)/shard_map/pallas_call | solution.py:182
  29.8 1.0 collective-permute-start.6
  30.8 1.6 %collective-permute-start = (bf16[64,2048]{1,0:T(8,128)(2,1)}, bf16[64,2048]{1,0:T(8,128)(2,1)S(1)}, u32[]{:S(2)}, u32[]{:S(2)}) collective-permute-start(bf16[64,2048]{1,0:T(8,128)(2,1)} %get-tuple-element.7), channel_id=1, source_target_pairs={{0,16},{16,32},{32,48},{48,0},{64,80},{80,96},{96,112},{112,64},{1... | collective-permute-start | bytes 786440 | tf_op jit(solution)/shard_map/ppermute | solution.py:36
  32.4 1.7 %collective-permute-start.1 = (bf16[64,2048]{1,0:T(8,128)(2,1)}, bf16[64,2048]{1,0:T(8,128)(2,1)S(1)}, u32[]{:S(2)}, u32[]{:S(2)}) collective-permute-start(bf16[64,2048]{1,0:T(8,128)(2,1)} %get-tuple-element.7), channel_id=1, source_target_pairs={{0,48},{16,0},{32,16},{48,32},{64,112},{80,64},{96,80},{112,96},{1... | collective-permute-start | bytes 786440 | tf_op jit(solution)/shard_map/ppermute | solution.py:36
  34.0 3.2 %collective-permute-done.6 = bf16[64,2048]{1,0:T(8,128)(2,1)S(1)} collective-permute-done((bf16[64,2048]{1,0:T(8,128)(2,1)}, bf16[64,2048]{1,0:T(8,128)(2,1)S(1)}, u32[]{:S(2)}, u32[]{:S(2)}) %collective-permute-start.6) | collective-permute-done | bytes 262176 | tf_op jit(solution)/shard_map/ppermute | solution.py:40
  37.3 1.0 fusion.29
  38.3 1.6 %collective-permute-start.7 = (bf16[2,64,2048]{2,1,0:T(8,128)(2,1)S(1)}, bf16[2,64,2048]{2,1,0:T(8,128)(2,1)S(1)}, u32[]{:S(2)}, u32[]{:S(2)}) collective-permute-start(bf16[2,64,2048]{2,1,0:T(8,128)(2,1)S(1)} %get-tuple-element.26), channel_id=1, source_target_pairs={{0,16},{16,32},{32,48},{48,0},{64,80},{80,96},{96,112},{112,64},{1... | collective-permute-start | bytes 1572872 | tf_op jit(solution)/shard_map/ppermute | solution.py:36
  39.9 1.0 constant_dynamic-update-slice_fusion.4
  40.9 1.7 %collective-permute-start.9 = (bf16[2,64,2048]{2,1,0:T(8,128)(2,1)S(1)}, bf16[2,64,2048]{2,1,0:T(8,128)(2,1)S(1)}, u32[]{:S(2)}, u32[]{:S(2)}) collective-permute-start(bf16[2,64,2048]{2,1,0:T(8,128)(2,1)S(1)} %get-tuple-element.26), channel_id=1, source_target_pairs={{0,48},{16,0},{32,16},{48,32},{64,112},{80,64},{96,80},{112,96},{1... | collective-permute-start | bytes 1572872 | tf_op jit(solution)/shard_map/ppermute | solution.py:36
  42.7 0.1 pad_maximum_fusion.3
  42.8 1.1 collective-permute-start.2
  43.9 0.4 collective-permute-start.3
  44.3 2.9 %collective-permute-start.4 = (bf16[32,2048]{1,0:T(8,128)(2,1)S(1)}, bf16[32,2048]{1,0:T(8,128)(2,1)S(1)}, u32[]{:S(2)}, u32[]{:S(2)}) collective-permute-start(bf16[32,2048]{1,0:T(8,128)(2,1)S(1)} %slice.151), channel_id=1, source_target_pairs={{0,48},{16,0},{32,16},{48,32},{64,112},{80,64},{96,80},{112,96},{1... | collective-permute-start | bytes 393224 | tf_op jit(solution)/shard_map/ppermute | solution.py:36
  47.3 5.9 %collective-permute-done.7 = bf16[2,64,2048]{2,1,0:T(8,128)(2,1)S(1)} collective-permute-done((bf16[2,64,2048]{2,1,0:T(8,128)(2,1)S(1)}, bf16[2,64,2048]{2,1,0:T(8,128)(2,1)S(1)}, u32[]{:S(2)}, u32[]{:S(2)}) %collective-permute-start.7) | collective-permute-done | bytes 524320 | tf_op jit(solution)/shard_map/ppermute | solution.py:36
  53.2 1.6 %collective-permute-start.8 = (bf16[64,2048]{1,0:T(8,128)(2,1)S(1)}, bf16[64,2048]{1,0:T(8,128)(2,1)S(1)}, u32[]{:S(2)}, u32[]{:S(2)}) collective-permute-start(bf16[64,2048]{1,0:T(8,128)(2,1)S(1)} %slice_bitcast_fusion.1), channel_id=1, source_target_pairs={{0,16},{16,32},{32,48},{48,0},{64,80},{80,96},{96,112},{112,64},{1... | collective-permute-start | bytes 786440 | tf_op jit(solution)/shard_map/ppermute | solution.py:36
  54.8 1.0 collective-permute-done.9
  55.8 1.8 %collective-permute-start.10 = (bf16[64,2048]{1,0:T(8,128)(2,1)S(1)}, bf16[64,2048]{1,0:T(8,128)(2,1)S(1)}, u32[]{:S(2)}, u32[]{:S(2)}) collective-permute-start(bf16[64,2048]{1,0:T(8,128)(2,1)S(1)} %slice_bitcast_fusion), channel_id=1, source_target_pairs={{0,48},{16,0},{32,16},{48,32},{64,112},{80,64},{96,80},{112,96},{1... | collective-permute-start | bytes 786440 | tf_op jit(solution)/shard_map/ppermute | solution.py:36
  57.6 0.8 collective-permute-done.4
  58.4 1.1 collective-permute-start.5
  59.5 1.4 collective-permute-done.8
  60.9 1.4 collective-permute-done.10
  62.2 0.1 maximum_bitcast_fusion
  62.3 0.0 slice-start.1
  62.3 0.3 pad_maximum_fusion
  62.6 6.4 %fusion.19 = bf16[512,1536]{1,0:T(8,128)(2,1)S(1)} fusion(bf16[512,2048]{1,0:T(8,128)(2,1)S(1)} %bitcast.66, bf16[4096,2048]{1,0:T(8,128)(2,1)} %param.13), kind=kOutput, calls=%fused_computation.12 | convolution fusion | flops 3222011904 | bytes 9961472 | tf_op jit(solution)/shard_map/dot_general | solution.py:216
  69.0 0.3 collective-permute-start.11
  69.3 7.0 %fusion.10 = bf16[512,2560]{1,0:T(8,128)(2,1)} fusion(bf16[512,2048]{1,0:T(8,128)(2,1)S(1)} %bitcast.67, bf16[4096,2048]{1,0:T(8,128)(2,1)S(1)} %bitcast.82), kind=kOutput, calls=%fused_computation.9 | convolution fusion | flops 5370019840 | bytes 15204352 | tf_op jit(solution)/shard_map/dot_general | solution.py:216
  76.3 0.5 collective-permute-start.17
  77.0 3.4 %fusion.16 = bf16[512,1536]{1,0:T(8,128)(2,1)S(1)} fusion(bf16[512,1536]{1,0:T(8,128)(2,1)S(1)} %collective-permute-done.11, bf16[512,2048]{1,0:T(8,128)(2,1)S(1)} %bitcast.79, bf16[4096,2048]{1,0:T(8,128)(2,1)S(1)} %bitcast.82), kind=kOutput, calls=%fused_computation.11 | convolution fusion | flops 3223584768 | bytes 11534336 | tf_op jit(solution)/shard_map/dot_general | solution.py:221
  80.4 0.1 dynamic-slice_bitcast_fusion
  80.5 1.6 %collective-permute-start.12 = (bf16[4,64,1536]{2,1,0:T(8,128)(2,1)S(1)}, bf16[4,64,1536]{2,1,0:T(8,128)(2,1)S(1)}, u32[]{:S(2)}, u32[]{:S(2)}) collective-permute-start(bf16[4,64,1536]{2,1,0:T(8,128)(2,1)S(1)} %dynamic-slice_bitcast_fusion), channel_id=1, source_target_pairs={{0,8},{1,9},{2,10},{3,11},{4,12},{5,13},{6,14},{7,15},{8,0},{9,1},... | collective-permute-start | bytes 2359304 | tf_op jit(solution)/shard_map/ppermute | solution.py:28
  82.1 19.4 %collective-permute-done.12 = bf16[4,64,1536]{2,1,0:T(8,128)(2,1)S(1)} collective-permute-done((bf16[4,64,1536]{2,1,0:T(8,128)(2,1)S(1)}, bf16[4,64,1536]{2,1,0:T(8,128)(2,1)S(1)}, u32[]{:S(2)}, u32[]{:S(2)}) %collective-permute-start.12) | collective-permute-done | bytes 786464 | tf_op jit(solution)/shard_map/ppermute | solution.py:28
  101.6 0.2 fusion.22
  101.8 10.2 %add_convert_fusion = bf16[512,2560]{1,0:T(8,128)(2,1)S(1)} fusion(bf16[512,2560]{1,0:T(8,128)(2,1)} %collective-permute-done.17, bf16[512,2048]{1,0:T(8,128)(2,1)S(1)} %bitcast.80, bf16[4096,2048]{1,0:T(8,128)(2,1)} %param.13), kind=kOutput, calls=%fused_computation.8 | convolution fusion | flops 5372641280 | bytes 17825792 | tf_op jit(solution)/shard_map/dot_general | solution.py:221
  112.0 0.1 constant_dynamic-slice_fusion.4
  112.2 0.1 pad_maximum_fusion.4
  112.2 2.5 %collective-permute-start.18 = (bf16[2,64,2560]{2,1,0:T(8,128)(2,1)S(1)}, bf16[2,64,2560]{2,1,0:T(8,128)(2,1)S(1)}, u32[]{:S(2)}, u32[]{:S(2)}) collective-permute-start(bf16[2,64,2560]{2,1,0:T(8,128)(2,1)S(1)} %pad_maximum_fusion.4), channel_id=1, source_target_pairs={{0,6},{1,7},{2,0},{3,1},{4,2},{5,3},{6,4},{7,5},{8,14},{9,15},{10,... | collective-permute-start | bytes 1966088 | tf_op jit(solution)/shard_map/ppermute | solution.py:24
  114.7 0.1 pad_maximum_fusion.5
  114.8 0.1 collective-permute-start.19
  114.9 3.3 %collective-permute-start.13 = (bf16[2,32,1536]{2,1,0:T(8,128)(2,1)S(1)}, bf16[2,32,1536]{2,1,0:T(8,128)(2,1)S(1)}, u32[]{:S(2)}, u32[]{:S(2)}) collective-permute-start(bf16[2,32,1536]{2,1,0:T(8,128)(2,1)S(1)} %pad_maximum_fusion.7), channel_id=1, source_target_pairs={{0,6},{1,7},{2,0},{3,1},{4,2},{5,3},{6,4},{7,5},{8,14},{9,15},{10,... | collective-permute-start | bytes 589832 | tf_op jit(solution)/shard_map/ppermute | solution.py:24
  118.2 0.1 collective-permute-start.14
  118.3 11.6 %collective-permute-done.18 = bf16[2,64,2560]{2,1,0:T(8,128)(2,1)S(1)} collective-permute-done((bf16[2,64,2560]{2,1,0:T(8,128)(2,1)S(1)}, bf16[2,64,2560]{2,1,0:T(8,128)(2,1)S(1)}, u32[]{:S(2)}, u32[]{:S(2)}) %collective-permute-start.18) | collective-permute-done | bytes 655392 | tf_op jit(solution)/shard_map/ppermute | solution.py:24
  129.9 3.8 %collective-permute-done.19 = bf16[2,64,2560]{2,1,0:T(8,128)(2,1)S(1)} collective-permute-done((bf16[2,64,2560]{2,1,0:T(8,128)(2,1)S(1)}, bf16[2,64,2560]{2,1,0:T(8,128)(2,1)S(1)}, u32[]{:S(2)}, u32[]{:S(2)}) %collective-permute-start.19) | collective-permute-done | bytes 655392 | tf_op jit(solution)/shard_map/ppermute | solution.py:24
  133.7 0.2 fusion.23
  133.8 0.1 collective-permute-start.20
  133.9 3.2 %collective-permute-start.21 = (bf16[64,2560]{1,0:T(8,128)(2,1)S(1)}, bf16[64,2560]{1,0:T(8,128)(2,1)S(1)}, u32[]{:S(2)}, u32[]{:S(2)}) collective-permute-start(bf16[64,2560]{1,0:T(8,128)(2,1)S(1)} %get-tuple-element.12), channel_id=1, source_target_pairs={{0,6},{1,7},{2,0},{3,1},{4,2},{5,3},{6,4},{7,5},{8,14},{9,15},{10,... | collective-permute-start | bytes 983048 | tf_op jit(solution)/shard_map/ppermute | solution.py:24
  137.1 0.7 collective-permute-done.14
  137.9 0.1 fusion.26
  137.9 0.1 collective-permute-start.15
  138.0 3.2 %collective-permute-start.16 = (bf16[32,1536]{1,0:T(8,128)(2,1)S(1)}, bf16[32,1536]{1,0:T(8,128)(2,1)S(1)}, u32[]{:S(2)}, u32[]{:S(2)}) collective-permute-start(bf16[32,1536]{1,0:T(8,128)(2,1)S(1)} %get-tuple-element.20), channel_id=1, source_target_pairs={{0,6},{1,7},{2,0},{3,1},{4,2},{5,3},{6,4},{7,5},{8,14},{9,15},{10,... | collective-permute-start | bytes 294920 | tf_op jit(solution)/shard_map/ppermute | solution.py:24
  141.2 2.7 %collective-permute-done.20 = bf16[64,2560]{1,0:T(8,128)(2,1)S(1)} collective-permute-done((bf16[64,2560]{1,0:T(8,128)(2,1)S(1)}, bf16[64,2560]{1,0:T(8,128)(2,1)S(1)}, u32[]{:S(2)}, u32[]{:S(2)}) %collective-permute-start.20) | collective-permute-done | bytes 327712 | tf_op jit(solution)/shard_map/ppermute | solution.py:24
  143.9 0.2 bitcast_add_fusion.2
  144.1 0.1 pad_maximum_fusion.1
  144.3 0.6 collective-permute-start.22
  144.9 0.0 collective-permute-done.15
  144.9 0.1 bitcast_add_fusion.4
  145.0 7.9 %collective-permute-done.22 = bf16[64,2560]{1,0:T(8,128)(2,1)S(1)} collective-permute-done((bf16[64,2560]{1,0:T(8,128)(2,1)S(1)}, bf16[64,2560]{1,0:T(8,128)(2,1)S(1)}, u32[]{:S(2)}, u32[]{:S(2)}) %collective-permute-start.22) | collective-permute-done | bytes 327712 | tf_op jit(solution)/shard_map/ppermute | solution.py:28
  152.9 0.1 bitcast_add_fusion
  153.0 1.0 pad_maximum_fusion.2
  (46 shorter events, 0.4 us)
Async XLA Ops:
  0.0 13.0 %copy-start.5 = (s32[2]{0:T(128)S(1)}, s32[2]{0:T(128)}, u32[]{:S(2)}) copy-start(s32[2]{0:T(128)} %param.10) | copy-start | bytes 28
  0.0 13.0 %copy-start.4 = (f32[4]{0:T(128)S(1)}, f32[4]{0:T(128)}, u32[]{:S(2)}) copy-start(f32[4]{0:T(128)} %param.11) | copy-start | bytes 52
  5.1 20.2 %all-to-all-start = ((bf16[16,8,16,128]{3,2,1,0:T(8,128)(2,1)}), bf16[16,8,16,128]{3,2,1,0:T(8,128)(2,1)S(1)}, u32[]{:S(2)}, u32[]{:S(2)}) async-start(bf16[16,8,16,128]{3,2,1,0:T(8,128)(2,1)} %shard_map.73), calls=%async_computation | async-start | bytes 1048576 | tf_op jit(solution)/shard_map/all_to_all | solution.py:206
  25.3 0.8 copy-start
  29.8 12.9 %copy-start.1 = (bf16[64,2048]{1,0:T(8,128)(2,1)S(1)}, bf16[64,2048]{1,0:T(8,128)(2,1)}, u32[]{:S(2)}) copy-start(bf16[64,2048]{1,0:T(8,128)(2,1)} %get-tuple-element.7) | copy-start | bytes 786436
  29.8 7.5 %collective-permute-start.6 = (bf16[64,2048]{1,0:T(8,128)(2,1)}, bf16[64,2048]{1,0:T(8,128)(2,1)S(1)}, u32[]{:S(2)}, u32[]{:S(2)}) collective-permute-start(bf16[64,2048]{1,0:T(8,128)(2,1)} %get-tuple-element.8), channel_id=1, source_target_pairs={{0,64},{16,80},{32,96},{48,112},{64,0},{80,16},{96,32},{112,48},{1... | collective-permute-start | bytes 786440 | tf_op jit(solution)/shard_map/ppermute | solution.py:40
  30.8 11.9 %collective-permute-start = (bf16[64,2048]{1,0:T(8,128)(2,1)}, bf16[64,2048]{1,0:T(8,128)(2,1)S(1)}, u32[]{:S(2)}, u32[]{:S(2)}) collective-permute-start(bf16[64,2048]{1,0:T(8,128)(2,1)} %get-tuple-element.7), channel_id=1, source_target_pairs={{0,16},{16,32},{32,48},{48,0},{64,80},{80,96},{96,112},{112,64},{1... | collective-permute-start | bytes 786440 | tf_op jit(solution)/shard_map/ppermute | solution.py:36
  32.4 10.3 %collective-permute-start.1 = (bf16[64,2048]{1,0:T(8,128)(2,1)}, bf16[64,2048]{1,0:T(8,128)(2,1)S(1)}, u32[]{:S(2)}, u32[]{:S(2)}) collective-permute-start(bf16[64,2048]{1,0:T(8,128)(2,1)} %get-tuple-element.7), channel_id=1, source_target_pairs={{0,48},{16,0},{32,16},{48,32},{64,112},{80,64},{96,80},{112,96},{1... | collective-permute-start | bytes 786440 | tf_op jit(solution)/shard_map/ppermute | solution.py:36
  38.3 14.9 %collective-permute-start.7 = (bf16[2,64,2048]{2,1,0:T(8,128)(2,1)S(1)}, bf16[2,64,2048]{2,1,0:T(8,128)(2,1)S(1)}, u32[]{:S(2)}, u32[]{:S(2)}) collective-permute-start(bf16[2,64,2048]{2,1,0:T(8,128)(2,1)S(1)} %get-tuple-element.26), channel_id=1, source_target_pairs={{0,16},{16,32},{32,48},{48,0},{64,80},{80,96},{96,112},{112,64},{1... | collective-permute-start | bytes 1572872 | tf_op jit(solution)/shard_map/ppermute | solution.py:36
  40.9 14.9 %collective-permute-start.9 = (bf16[2,64,2048]{2,1,0:T(8,128)(2,1)S(1)}, bf16[2,64,2048]{2,1,0:T(8,128)(2,1)S(1)}, u32[]{:S(2)}, u32[]{:S(2)}) collective-permute-start(bf16[2,64,2048]{2,1,0:T(8,128)(2,1)S(1)} %get-tuple-element.26), channel_id=1, source_target_pairs={{0,48},{16,0},{32,16},{48,32},{64,112},{80,64},{96,80},{112,96},{1... | collective-permute-start | bytes 1572872 | tf_op jit(solution)/shard_map/ppermute | solution.py:36
  42.7 26.6 %slice-start = ((s8[16777216]{0:T(1024)(128)(4,1)}), s8[4194304]{0:T(1024)(128)(4,1)S(1)}, s32[]{:S(2)}) async-start(s8[16777216]{0:T(1024)(128)(4,1)} %bitcast.81), calls=%async_computation.1 | async-start | bytes 8388608
  42.8 34.0 %collective-permute-start.2 = (bf16[3,64,2048]{2,1,0:T(8,128)(2,1)S(1)}, bf16[3,64,2048]{2,1,0:T(8,128)(2,1)S(1)}, u32[]{:S(2)}, u32[]{:S(2)}) collective-permute-start(bf16[3,64,2048]{2,1,0:T(8,128)(2,1)S(1)} %pad_maximum_fusion.3), channel_id=1, source_target_pairs={{0,64},{16,80},{32,96},{48,112},{64,0},{80,16},{96,32},{112,48},{1... | collective-permute-start | bytes 2359304 | tf_op jit(solution)/shard_map/ppermute | solution.py:40
  43.9 13.7 %collective-permute-start.3 = (bf16[32,2048]{1,0:T(8,128)(2,1)S(1)}, bf16[32,2048]{1,0:T(8,128)(2,1)S(1)}, u32[]{:S(2)}, u32[]{:S(2)}) collective-permute-start(bf16[32,2048]{1,0:T(8,128)(2,1)S(1)} %slice.150), channel_id=1, source_target_pairs={{0,16},{16,32},{32,48},{48,0},{64,80},{80,96},{96,112},{112,64},{1... | collective-permute-start | bytes 393224 | tf_op jit(solution)/shard_map/ppermute | solution.py:36
  44.3 14.0 %collective-permute-start.4 = (bf16[32,2048]{1,0:T(8,128)(2,1)S(1)}, bf16[32,2048]{1,0:T(8,128)(2,1)S(1)}, u32[]{:S(2)}, u32[]{:S(2)}) collective-permute-start(bf16[32,2048]{1,0:T(8,128)(2,1)S(1)} %slice.151), channel_id=1, source_target_pairs={{0,48},{16,0},{32,16},{48,32},{64,112},{80,64},{96,80},{112,96},{1... | collective-permute-start | bytes 393224 | tf_op jit(solution)/shard_map/ppermute | solution.py:36
  53.2 7.7 %collective-permute-start.8 = (bf16[64,2048]{1,0:T(8,128)(2,1)S(1)}, bf16[64,2048]{1,0:T(8,128)(2,1)S(1)}, u32[]{:S(2)}, u32[]{:S(2)}) collective-permute-start(bf16[64,2048]{1,0:T(8,128)(2,1)S(1)} %slice_bitcast_fusion.1), channel_id=1, source_target_pairs={{0,16},{16,32},{32,48},{48,0},{64,80},{80,96},{96,112},{112,64},{1... | collective-permute-start | bytes 786440 | tf_op jit(solution)/shard_map/ppermute | solution.py:36
  55.8 6.4 %collective-permute-start.10 = (bf16[64,2048]{1,0:T(8,128)(2,1)S(1)}, bf16[64,2048]{1,0:T(8,128)(2,1)S(1)}, u32[]{:S(2)}, u32[]{:S(2)}) collective-permute-start(bf16[64,2048]{1,0:T(8,128)(2,1)S(1)} %slice_bitcast_fusion), channel_id=1, source_target_pairs={{0,48},{16,0},{32,16},{48,32},{64,112},{80,64},{96,80},{112,96},{1... | collective-permute-start | bytes 786440 | tf_op jit(solution)/shard_map/ppermute | solution.py:36
  58.4 18.5 %collective-permute-start.5 = (bf16[64,2048]{1,0:T(8,128)(2,1)S(1)}, bf16[64,2048]{1,0:T(8,128)(2,1)S(1)}, u32[]{:S(2)}, u32[]{:S(2)}) collective-permute-start(bf16[64,2048]{1,0:T(8,128)(2,1)S(1)} %constant_dynamic-update-slice_fusion), channel_id=1, source_target_pairs={{0,64},{16,80},{32,96},{48,112},{64,0},{80,16},{96,32},{112,48},{1... | collective-permute-start | bytes 786440 | tf_op jit(solution)/shard_map/ppermute | solution.py:40
  62.3 7.0 %slice-start.1 = ((s8[16777216]{0:T(1024)(128)(4,1)}), s8[4194304]{0:T(1024)(128)(4,1)S(1)}, s32[]{:S(2)}) async-start(s8[16777216]{0:T(1024)(128)(4,1)} %bitcast.81), calls=%async_computation.2 | async-start | bytes 8388608
  62.6 6.7 %slice-start.2 = ((s8[16777216]{0:T(1024)(128)(4,1)}), s8[4194304]{0:T(1024)(128)(4,1)S(1)}, s32[]{:S(2)}) async-start(s8[16777216]{0:T(1024)(128)(4,1)} %bitcast.81), calls=%async_computation.3 | async-start | bytes 8388608
  62.6 6.7 %slice-start.3 = ((s8[16777216]{0:T(1024)(128)(4,1)}), s8[4194304]{0:T(1024)(128)(4,1)S(1)}, s32[]{:S(2)}) async-start(s8[16777216]{0:T(1024)(128)(4,1)} %bitcast.81), calls=%async_computation.4 | async-start | bytes 8388608
  69.0 8.0 %collective-permute-start.11 = (bf16[512,1536]{1,0:T(8,128)(2,1)S(1)}, bf16[512,1536]{1,0:T(8,128)(2,1)S(1)}, u32[]{:S(2)}, u32[]{:S(2)}) collective-permute-start(bf16[512,1536]{1,0:T(8,128)(2,1)S(1)} %fusion.19), channel_id=1, source_target_pairs={{0,1},{1,0},{2,3},{3,2},{4,5},{5,4},{6,7},{7,6},{8,9},{9,8},{10,11... | collective-permute-start | bytes 4718600 | tf_op jit(solution)/shard_map/ppermute | solution.py:32
  76.3 25.5 %collective-permute-start.17 = (bf16[512,2560]{1,0:T(8,128)(2,1)}, bf16[512,2560]{1,0:T(8,128)(2,1)}, u32[]{:S(2)}, u32[]{:S(2)}) collective-permute-start(bf16[512,2560]{1,0:T(8,128)(2,1)} %fusion.10), channel_id=1, source_target_pairs={{0,1},{1,0},{2,3},{3,2},{4,5},{5,4},{6,7},{7,6},{8,9},{9,8},{10,11... | collective-permute-start | bytes 7864328 | tf_op jit(solution)/shard_map/ppermute | solution.py:32
  76.9 3.5 %copy-start.2 = (bf16[8,64,2048]{2,1,0:T(8,128)(2,1)}, bf16[8,64,2048]{2,1,0:T(8,128)(2,1)S(1)}, u32[]{:S(2)}) copy-start(bf16[8,64,2048]{2,1,0:T(8,128)(2,1)S(1)} %slice_dynamic-update-slice_fusion) | copy-start | bytes 6291460
  80.5 21.1 %collective-permute-start.12 = (bf16[4,64,1536]{2,1,0:T(8,128)(2,1)S(1)}, bf16[4,64,1536]{2,1,0:T(8,128)(2,1)S(1)}, u32[]{:S(2)}, u32[]{:S(2)}) collective-permute-start(bf16[4,64,1536]{2,1,0:T(8,128)(2,1)S(1)} %dynamic-slice_bitcast_fusion), channel_id=1, source_target_pairs={{0,8},{1,9},{2,10},{3,11},{4,12},{5,13},{6,14},{7,15},{8,0},{9,1},... | collective-permute-start | bytes 2359304 | tf_op jit(solution)/shard_map/ppermute | solution.py:28
  82.1 19.7 %copy-start.3 = (bf16[8,64,2048]{2,1,0:T(8,128)(2,1)S(1)}, bf16[8,64,2048]{2,1,0:T(8,128)(2,1)}, u32[]{:S(2)}) copy-start(bf16[8,64,2048]{2,1,0:T(8,128)(2,1)} %copy-done.2) | copy-start | bytes 6291460
  112.2 17.7 %collective-permute-start.18 = (bf16[2,64,2560]{2,1,0:T(8,128)(2,1)S(1)}, bf16[2,64,2560]{2,1,0:T(8,128)(2,1)S(1)}, u32[]{:S(2)}, u32[]{:S(2)}) collective-permute-start(bf16[2,64,2560]{2,1,0:T(8,128)(2,1)S(1)} %pad_maximum_fusion.4), channel_id=1, source_target_pairs={{0,6},{1,7},{2,0},{3,1},{4,2},{5,3},{6,4},{7,5},{8,14},{9,15},{10,... | collective-permute-start | bytes 1966088 | tf_op jit(solution)/shard_map/ppermute | solution.py:24
  114.8 18.9 %collective-permute-start.19 = (bf16[2,64,2560]{2,1,0:T(8,128)(2,1)S(1)}, bf16[2,64,2560]{2,1,0:T(8,128)(2,1)S(1)}, u32[]{:S(2)}, u32[]{:S(2)}) collective-permute-start(bf16[2,64,2560]{2,1,0:T(8,128)(2,1)S(1)} %pad_maximum_fusion.5), channel_id=1, source_target_pairs={{0,2},{1,3},{2,4},{3,5},{4,6},{5,7},{6,0},{7,1},{8,10},{9,11},{10,... | collective-permute-start | bytes 1966088 | tf_op jit(solution)/shard_map/ppermute | solution.py:24
  114.9 22.2 %collective-permute-start.13 = (bf16[2,32,1536]{2,1,0:T(8,128)(2,1)S(1)}, bf16[2,32,1536]{2,1,0:T(8,128)(2,1)S(1)}, u32[]{:S(2)}, u32[]{:S(2)}) collective-permute-start(bf16[2,32,1536]{2,1,0:T(8,128)(2,1)S(1)} %pad_maximum_fusion.7), channel_id=1, source_target_pairs={{0,6},{1,7},{2,0},{3,1},{4,2},{5,3},{6,4},{7,5},{8,14},{9,15},{10,... | collective-permute-start | bytes 589832 | tf_op jit(solution)/shard_map/ppermute | solution.py:24
  118.2 19.6 %collective-permute-start.14 = (bf16[2,32,1536]{2,1,0:T(8,128)(2,1)S(1)}, bf16[2,32,1536]{2,1,0:T(8,128)(2,1)S(1)}, u32[]{:S(2)}, u32[]{:S(2)}) collective-permute-start(bf16[2,32,1536]{2,1,0:T(8,128)(2,1)S(1)} %pad_maximum_fusion.8), channel_id=1, source_target_pairs={{0,2},{1,3},{2,4},{3,5},{4,6},{5,7},{6,0},{7,1},{8,10},{9,11},{10,... | collective-permute-start | bytes 589832 | tf_op jit(solution)/shard_map/ppermute | solution.py:24
  133.8 10.1 %collective-permute-start.20 = (bf16[64,2560]{1,0:T(8,128)(2,1)S(1)}, bf16[64,2560]{1,0:T(8,128)(2,1)S(1)}, u32[]{:S(2)}, u32[]{:S(2)}) collective-permute-start(bf16[64,2560]{1,0:T(8,128)(2,1)S(1)} %get-tuple-element.11), channel_id=1, source_target_pairs={{0,2},{1,3},{2,4},{3,5},{4,6},{5,7},{6,0},{7,1},{8,10},{9,11},{10,... | collective-permute-start | bytes 983048 | tf_op jit(solution)/shard_map/ppermute | solution.py:24
  133.9 10.0 %collective-permute-start.21 = (bf16[64,2560]{1,0:T(8,128)(2,1)S(1)}, bf16[64,2560]{1,0:T(8,128)(2,1)S(1)}, u32[]{:S(2)}, u32[]{:S(2)}) collective-permute-start(bf16[64,2560]{1,0:T(8,128)(2,1)S(1)} %get-tuple-element.12), channel_id=1, source_target_pairs={{0,6},{1,7},{2,0},{3,1},{4,2},{5,3},{6,4},{7,5},{8,14},{9,15},{10,... | collective-permute-start | bytes 983048 | tf_op jit(solution)/shard_map/ppermute | solution.py:24
  137.9 7.0 %collective-permute-start.15 = (bf16[32,1536]{1,0:T(8,128)(2,1)S(1)}, bf16[32,1536]{1,0:T(8,128)(2,1)S(1)}, u32[]{:S(2)}, u32[]{:S(2)}) collective-permute-start(bf16[32,1536]{1,0:T(8,128)(2,1)S(1)} %get-tuple-element.19), channel_id=1, source_target_pairs={{0,2},{1,3},{2,4},{3,5},{4,6},{5,7},{6,0},{7,1},{8,10},{9,11},{10,... | collective-permute-start | bytes 294920 | tf_op jit(solution)/shard_map/ppermute | solution.py:24
  138.0 6.9 %collective-permute-start.16 = (bf16[32,1536]{1,0:T(8,128)(2,1)S(1)}, bf16[32,1536]{1,0:T(8,128)(2,1)S(1)}, u32[]{:S(2)}, u32[]{:S(2)}) collective-permute-start(bf16[32,1536]{1,0:T(8,128)(2,1)S(1)} %get-tuple-element.20), channel_id=1, source_target_pairs={{0,6},{1,7},{2,0},{3,1},{4,2},{5,3},{6,4},{7,5},{8,14},{9,15},{10,... | collective-permute-start | bytes 294920 | tf_op jit(solution)/shard_map/ppermute | solution.py:24
  144.3 8.7 %collective-permute-start.22 = (bf16[64,2560]{1,0:T(8,128)(2,1)S(1)}, bf16[64,2560]{1,0:T(8,128)(2,1)S(1)}, u32[]{:S(2)}, u32[]{:S(2)}) collective-permute-start(bf16[64,2560]{1,0:T(8,128)(2,1)S(1)} %fusion.25), channel_id=1, source_target_pairs={{0,8},{1,9},{2,10},{3,11},{4,12},{5,13},{6,14},{7,15},{8,0},{9,1},... | collective-permute-start | bytes 983048 | tf_op jit(solution)/shard_map/ppermute | solution.py:28
where the time goes:
time: 155 us; the launch traced here: 154 us
  waiting for transfers between devices  71.4 us (46%)
  starting transfers between devices  39.9 us (26%)
  matrix products  27 us (17%)
  Pallas kernels  8.82 us (6%)
  other arithmetic  4.15 us (3%)
  local copies, waits for them, and re-layouts  2.28 us (1%)
    ppermute x2, waiting for transfers between devices, over_z_hi(): return lax.ppermute(v, 'mod', mod_perm(1, 0, 0))  27.3 us
    ppermute x8, waiting for transfers between devices, over_x(): return lax.ppermute(v, 'mod', mod_perm(0, step, 0))  18.8 us
    dot_general x2, matrix products, compute(): lax.dot_general(own_rows, stored[n], dims, preferred_element_type=jnp.flo...  13.7 us
    ppermute x8, starting transfers between devices, over_y(): return lax.ppermute(v, 'store', store_perm(0, step))  13.3 us
    dot_general x2, matrix products, compute(): lax.dot_general(sibling_rows, stored[n], dims, preferred_element_type=jnp...  13.3 us
    ppermute x8, starting transfers between devices, over_x(): return lax.ppermute(v, 'mod', mod_perm(0, step, 0))  12.5 us
    all_to_all x1, waiting for transfers between devices, compute(): lax.all_to_all(per_sample, 'mod', split_axis=0, concat_axis=0, tiled=True)  11.6 us
    ppermute x8, waiting for transfers between devices, over_y(): return lax.ppermute(v, 'store', store_perm(0, step))  10.4 us
  transfers between devices with their start and end apart: 24, of which 13 were waited for; matrix products, arithmetic and copies ran while one was open for 14% of the time, Pallas kernels for 0%

commit v1 on v0

--- a/solution.py
+++ b/solution.py
@@ -147,30 +147,25 @@
     )(token_mask, grad_proj, act_proj)
 
 
-def fisher_kernel(core_ref, weight_ref, rows_ref, fisher_ref, sibling_ref, own_ref, wide_ref):
-    module = pl.program_id(0)
-
-    @pl.when(module == 0)
-    def _():
-        wide_ref[...] = rows_ref[...].reshape(wide_ref.shape).astype(jnp.float32)
-
+def fisher_kernel(core_ref, weight_ref, rows_ref, fisher_ref, sibling_ref, own_ref, wide_ref, near_ref, semaphores):
+    modules = fisher_ref.shape[0]
+    copies = [pltpu.make_async_copy(fisher_ref.at[m], near_ref.at[m], semaphores.at[m]) for m in range(modules)]
+    for copy in copies:
+        copy.start()
+    wide_ref[...] = rows_ref[...].reshape(wide_ref.shape).astype(jnp.float32)
     count = wide_ref.shape[0] // 16
-    pieces = [wide_ref[pl.ds(module * 8 + r, count, stride=16), :] for r in range(8)]
-    left = jnp.concatenate(pieces, axis=1).astype(jnp.bfloat16)
-    product = jnp.dot(left, fisher_ref[0], preferred_element_type=jnp.float32)
-    scaled = (product * weight_ref[module]).astype(jnp.bfloat16)
+    half = count // 2
     first = core_ref[0] == 0
-    half = count // 2
-
-    @pl.when(first)
-    def _():
-        own_ref[...] = scaled[:half]
-        sibling_ref[...] = scaled[half:]
-
-    @pl.when(jnp.logical_not(first))
-    def _():
-        own_ref[...] = scaled[half:]
-        sibling_ref[...] = scaled[:half]
+    rank = fisher_ref.shape[1]
+    for m in range(modules):
+        pieces = [wide_ref[pl.ds(m * 8 + r, count, stride=16), :] for r in range(8)]
+        left = jnp.concatenate(pieces, axis=1).astype(jnp.bfloat16)
+        copies[m].wait()
+        product = jnp.dot(left, near_ref[m], preferred_element_type=jnp.float32)
+        scaled = (product * weight_ref[m]).astype(jnp.bfloat16)
+        columns = slice(m * rank, m * rank + rank)
+        own_ref[:, columns] = jnp.where(first, scaled[:half], scaled[half:])
+        sibling_ref[:, columns] = jnp.where(first, scaled[half:], scaled[:half])
 
 
 def conditioned_rows(core, module_weight, grouped, fisher_inv):
@@ -178,19 +173,18 @@
     modules, rank = fisher_inv.shape[:2]
     count = sources * queries
     out = jax.ShapeDtypeStruct((count // 2, modules * rank), jnp.bfloat16)
-    out_spec = pl.BlockSpec((count // 2, rank), lambda m: (0, m))
+    near = pl.BlockSpec(memory_space=pltpu.VMEM)
+    scalars = pl.BlockSpec(memory_space=pltpu.SMEM)
     return pl.pallas_call(
         fisher_kernel,
-        grid=(modules,),
-        in_specs=[
-            pl.BlockSpec(memory_space=pltpu.SMEM),
-            pl.BlockSpec(memory_space=pltpu.SMEM),
-            pl.BlockSpec(memory_space=pltpu.VMEM),
-            pl.BlockSpec((1, rank, rank), lambda m: (m, 0, 0)),
+        in_specs=[scalars, scalars, near, pl.BlockSpec(memory_space=pl.ANY)],
+        out_specs=[near, near],
+        out_shape=[out, out],
+        scratch_shapes=[
+            pltpu.VMEM((count * 16, 128), jnp.float32),
+            pltpu.VMEM(fisher_inv.shape, jnp.bfloat16),
+            pltpu.SemaphoreType.DMA((modules,)),
         ],
-        out_specs=[out_spec, out_spec],
-        out_shape=[out, out],
-        scratch_shapes=[pltpu.VMEM((count * 16, 128), jnp.float32)],
     )(core[None], module_weight, grouped, fisher_inv)
 
 

time: 155 us -> 156 us (level)
  no operation moved by 1% of the time
where the time goes in v1:
time: 156 us; the launch traced here: 155 us
  waiting for transfers between devices  71.5 us (46%)
  starting transfers between devices  39.9 us (26%)
  matrix products  27 us (17%)
  Pallas kernels  9.68 us (6%)
  other arithmetic  4.15 us (3%)
  local copies, waits for them, and re-layouts  2.28 us (1%)
    ppermute x2, waiting for transfers between devices, over_z_hi(): return lax.ppermute(v, 'mod', mod_perm(1, 0, 0))  27.3 us
    ppermute x8, waiting for transfers between devices, over_x(): return lax.ppermute(v, 'mod', mod_perm(0, step, 0))  18.8 us
    dot_general x2, matrix products, compute(): lax.dot_general(own_rows, stored[n], dims, preferred_element_type=jnp.flo...  13.7 us
    ppermute x8, starting transfers between devices, over_y(): return lax.ppermute(v, 'store', store_perm(0, step))  13.3 us
    dot_general x2, matrix products, compute(): lax.dot_general(sibling_rows, stored[n], dims, preferred_element_type=jnp...  13.3 us
    ppermute x8, starting transfers between devices, over_x(): return lax.ppermute(v, 'mod', mod_perm(0, step, 0))  12.5 us
    all_to_all x1, waiting for transfers between devices, compute(): lax.all_to_all(per_sample, 'mod', split_axis=0, concat_axis=0, tiled=True)  11.6 us
    ppermute x8, waiting for transfers between devices, over_y(): return lax.ppermute(v, 'store', store_perm(0, step))  10.5 us
  transfers between devices with their start and end apart: 24, of which 13 were waited for; matrix products, arithmetic and copies ran while one was open for 14% of the time, Pallas kernels for 0%

profile of v1, /device:TPU:0, one launch (start us, length us, event | category | flops | bytes accessed | tf_op | source)
XLA Modules:
  0.0 155.0 jit_solution(3028946452819341353)
XLA Ops:
  0.0 5.1 %shard_map.73 = bf16[16,8,16,128]{3,2,1,0:T(8,128)(2,1)} custom-call(s32[8,256]{1,0:T(8,128)} %mask_ref.1, bf16[8,256,1024]{2,1,0:T(8,128)(2,1)} %grad_ref.1, bf16[8,256,1024]{2,1,0:T(8,128)(2,1)} %act_ref.1), custom_call_target="tpu_custom_call" | custom-call | tf_op jit(solution)/shard_map/pallas_call | solution.py:136
  5.1 7.8 %all-to-all-start = ((bf16[16,8,16,128]{3,2,1,0:T(8,128)(2,1)}), bf16[16,8,16,128]{3,2,1,0:T(8,128)(2,1)S(1)}, u32[]{:S(2)}, u32[]{:S(2)}) async-start(bf16[16,8,16,128]{3,2,1,0:T(8,128)(2,1)} %shard_map.73), calls=%async_computation | async-start | bytes 1048576 | tf_op jit(solution)/shard_map/all_to_all | solution.py:200
  13.0 0.7 fusion.28.weight_ref
  13.7 11.6 %all-to-all-done.rows_ref = bf16[16,8,16,128]{3,2,1,0:T(8,128)(2,1)S(1)} async-done(((bf16[16,8,16,128]{3,2,1,0:T(8,128)(2,1)}), bf16[16,8,16,128]{3,2,1,0:T(8,128)(2,1)S(1)}, u32[]{:S(2)}, u32[]{:S(2)}) %all-to-all-start) | async-done | bytes 524320 | tf_op jit(solution)/shard_map/all_to_all | solution.py:200
  25.3 0.8 copy-done
  26.1 4.6 %shard_map.74 = (bf16[64,2048]{1,0:T(8,128)(2,1)}, bf16[64,2048]{1,0:T(8,128)(2,1)}) custom-call(s32[1]{0:T(128)} %bitcast.core_ref, f32[2]{0:T(128)} %fusion.28.weight_ref, bf16[16,8,16,128]{3,2,1,0:T(8,128)(2,1)} %copy-done, bf16[2,1024,1024]{2,1,0:T(8,128)(2,1)} %fisher_ref.1), custom_call_target="tpu_custom_call" | custom-call | tf_op jit(solution)/shard_map/pallas_call | solution.py:178
  30.7 1.1 collective-permute-start.6
  31.8 1.6 %collective-permute-start = (bf16[64,2048]{1,0:T(8,128)(2,1)}, bf16[64,2048]{1,0:T(8,128)(2,1)S(1)}, u32[]{:S(2)}, u32[]{:S(2)}) collective-permute-start(bf16[64,2048]{1,0:T(8,128)(2,1)} %get-tuple-element.7), channel_id=1, source_target_pairs={{0,16},{16,32},{32,48},{48,0},{64,80},{80,96},{96,112},{112,64},{1... | collective-permute-start | bytes 786440 | tf_op jit(solution)/shard_map/ppermute | solution.py:36
  33.3 1.7 %collective-permute-start.1 = (bf16[64,2048]{1,0:T(8,128)(2,1)}, bf16[64,2048]{1,0:T(8,128)(2,1)S(1)}, u32[]{:S(2)}, u32[]{:S(2)}) collective-permute-start(bf16[64,2048]{1,0:T(8,128)(2,1)} %get-tuple-element.7), channel_id=1, source_target_pairs={{0,48},{16,0},{32,16},{48,32},{64,112},{80,64},{96,80},{112,96},{1... | collective-permute-start | bytes 786440 | tf_op jit(solution)/shard_map/ppermute | solution.py:36
  35.0 3.2 %collective-permute-done.6 = bf16[64,2048]{1,0:T(8,128)(2,1)S(1)} collective-permute-done((bf16[64,2048]{1,0:T(8,128)(2,1)}, bf16[64,2048]{1,0:T(8,128)(2,1)S(1)}, u32[]{:S(2)}, u32[]{:S(2)}) %collective-permute-start.6) | collective-permute-done | bytes 262176 | tf_op jit(solution)/shard_map/ppermute | solution.py:40
  38.3 1.0 fusion.29
  39.3 1.6 %collective-permute-start.7 = (bf16[2,64,2048]{2,1,0:T(8,128)(2,1)S(1)}, bf16[2,64,2048]{2,1,0:T(8,128)(2,1)S(1)}, u32[]{:S(2)}, u32[]{:S(2)}) collective-permute-start(bf16[2,64,2048]{2,1,0:T(8,128)(2,1)S(1)} %get-tuple-element.26), channel_id=1, source_target_pairs={{0,16},{16,32},{32,48},{48,0},{64,80},{80,96},{96,112},{112,64},{1... | collective-permute-start | bytes 1572872 | tf_op jit(solution)/shard_map/ppermute | solution.py:36
  40.9 1.0 constant_dynamic-update-slice_fusion.4
  41.9 1.7 %collective-permute-start.9 = (bf16[2,64,2048]{2,1,0:T(8,128)(2,1)S(1)}, bf16[2,64,2048]{2,1,0:T(8,128)(2,1)S(1)}, u32[]{:S(2)}, u32[]{:S(2)}) collective-permute-start(bf16[2,64,2048]{2,1,0:T(8,128)(2,1)S(1)} %get-tuple-element.26), channel_id=1, source_target_pairs={{0,48},{16,0},{32,16},{48,32},{64,112},{80,64},{96,80},{112,96},{1... | collective-permute-start | bytes 1572872 | tf_op jit(solution)/shard_map/ppermute | solution.py:36
  43.6 0.1 pad_maximum_fusion.3
  43.7 1.1 collective-permute-start.2
  44.8 0.4 collective-permute-start.3
  45.3 2.9 %collective-permute-start.4 = (bf16[32,2048]{1,0:T(8,128)(2,1)S(1)}, bf16[32,2048]{1,0:T(8,128)(2,1)S(1)}, u32[]{:S(2)}, u32[]{:S(2)}) collective-permute-start(bf16[32,2048]{1,0:T(8,128)(2,1)S(1)} %slice.151), channel_id=1, source_target_pairs={{0,48},{16,0},{32,16},{48,32},{64,112},{80,64},{96,80},{112,96},{1... | collective-permute-start | bytes 393224 | tf_op jit(solution)/shard_map/ppermute | solution.py:36
  48.2 5.9 %collective-permute-done.7 = bf16[2,64,2048]{2,1,0:T(8,128)(2,1)S(1)} collective-permute-done((bf16[2,64,2048]{2,1,0:T(8,128)(2,1)S(1)}, bf16[2,64,2048]{2,1,0:T(8,128)(2,1)S(1)}, u32[]{:S(2)}, u32[]{:S(2)}) %collective-permute-start.7) | collective-permute-done | bytes 524320 | tf_op jit(solution)/shard_map/ppermute | solution.py:36
  54.2 1.6 %collective-permute-start.8 = (bf16[64,2048]{1,0:T(8,128)(2,1)S(1)}, bf16[64,2048]{1,0:T(8,128)(2,1)S(1)}, u32[]{:S(2)}, u32[]{:S(2)}) collective-permute-start(bf16[64,2048]{1,0:T(8,128)(2,1)S(1)} %slice_bitcast_fusion.1), channel_id=1, source_target_pairs={{0,16},{16,32},{32,48},{48,0},{64,80},{80,96},{96,112},{112,64},{1... | collective-permute-start | bytes 786440 | tf_op jit(solution)/shard_map/ppermute | solution.py:36
  55.8 1.0 collective-permute-done.9
  56.8 1.8 %collective-permute-start.10 = (bf16[64,2048]{1,0:T(8,128)(2,1)S(1)}, bf16[64,2048]{1,0:T(8,128)(2,1)S(1)}, u32[]{:S(2)}, u32[]{:S(2)}) collective-permute-start(bf16[64,2048]{1,0:T(8,128)(2,1)S(1)} %slice_bitcast_fusion), channel_id=1, source_target_pairs={{0,48},{16,0},{32,16},{48,32},{64,112},{80,64},{96,80},{112,96},{1... | collective-permute-start | bytes 786440 | tf_op jit(solution)/shard_map/ppermute | solution.py:36
  58.5 0.8 collective-permute-done.4
  59.4 1.1 collective-permute-start.5
  60.5 1.4 collective-permute-done.8
  61.8 1.4 collective-permute-done.10
  63.2 0.1 maximum_bitcast_fusion
  63.3 0.3 pad_maximum_fusion
  63.5 0.0 slice-start.2
  63.6 6.4 %fusion.19 = bf16[512,1536]{1,0:T(8,128)(2,1)S(1)} fusion(bf16[512,2048]{1,0:T(8,128)(2,1)S(1)} %bitcast.66, bf16[4096,2048]{1,0:T(8,128)(2,1)} %param.13), kind=kOutput, calls=%fused_computation.12 | convolution fusion | flops 3222011904 | bytes 9961472 | tf_op jit(solution)/shard_map/dot_general | solution.py:210
  70.0 0.3 collective-permute-start.11
  70.3 7.0 %fusion.10 = bf16[512,2560]{1,0:T(8,128)(2,1)} fusion(bf16[512,2048]{1,0:T(8,128)(2,1)S(1)} %bitcast.67, bf16[4096,2048]{1,0:T(8,128)(2,1)S(1)} %bitcast.82), kind=kOutput, calls=%fused_computation.9 | convolution fusion | flops 5370019840 | bytes 15204352 | tf_op jit(solution)/shard_map/dot_general | solution.py:210
  77.2 0.5 collective-permute-start.17
  77.9 3.4 %fusion.16 = bf16[512,1536]{1,0:T(8,128)(2,1)S(1)} fusion(bf16[512,1536]{1,0:T(8,128)(2,1)S(1)} %collective-permute-done.11, bf16[512,2048]{1,0:T(8,128)(2,1)S(1)} %bitcast.79, bf16[4096,2048]{1,0:T(8,128)(2,1)S(1)} %bitcast.82), kind=kOutput, calls=%fused_computation.11 | convolution fusion | flops 3223584768 | bytes 11534336 | tf_op jit(solution)/shard_map/dot_general | solution.py:215
  81.4 0.1 dynamic-slice_bitcast_fusion
  81.5 1.6 %collective-permute-start.12 = (bf16[4,64,1536]{2,1,0:T(8,128)(2,1)S(1)}, bf16[4,64,1536]{2,1,0:T(8,128)(2,1)S(1)}, u32[]{:S(2)}, u32[]{:S(2)}) collective-permute-start(bf16[4,64,1536]{2,1,0:T(8,128)(2,1)S(1)} %dynamic-slice_bitcast_fusion), channel_id=1, source_target_pairs={{0,8},{1,9},{2,10},{3,11},{4,12},{5,13},{6,14},{7,15},{8,0},{9,1},... | collective-permute-start | bytes 2359304 | tf_op jit(solution)/shard_map/ppermute | solution.py:28
  83.1 19.4 %collective-permute-done.12 = bf16[4,64,1536]{2,1,0:T(8,128)(2,1)S(1)} collective-permute-done((bf16[4,64,1536]{2,1,0:T(8,128)(2,1)S(1)}, bf16[4,64,1536]{2,1,0:T(8,128)(2,1)S(1)}, u32[]{:S(2)}, u32[]{:S(2)}) %collective-permute-start.12) | collective-permute-done | bytes 786464 | tf_op jit(solution)/shard_map/ppermute | solution.py:28
  102.5 0.2 fusion.22
  102.7 10.2 %add_convert_fusion = bf16[512,2560]{1,0:T(8,128)(2,1)S(1)} fusion(bf16[512,2560]{1,0:T(8,128)(2,1)} %collective-permute-done.17, bf16[512,2048]{1,0:T(8,128)(2,1)S(1)} %bitcast.80, bf16[4096,2048]{1,0:T(8,128)(2,1)} %param.13), kind=kOutput, calls=%fused_computation.8 | convolution fusion | flops 5372641280 | bytes 17825792 | tf_op jit(solution)/shard_map/dot_general | solution.py:215
  113.0 0.1 constant_dynamic-slice_fusion.4
  113.1 0.1 pad_maximum_fusion.4
  113.2 2.5 %collective-permute-start.18 = (bf16[2,64,2560]{2,1,0:T(8,128)(2,1)S(1)}, bf16[2,64,2560]{2,1,0:T(8,128)(2,1)S(1)}, u32[]{:S(2)}, u32[]{:S(2)}) collective-permute-start(bf16[2,64,2560]{2,1,0:T(8,128)(2,1)S(1)} %pad_maximum_fusion.4), channel_id=1, source_target_pairs={{0,6},{1,7},{2,0},{3,1},{4,2},{5,3},{6,4},{7,5},{8,14},{9,15},{10,... | collective-permute-start | bytes 1966088 | tf_op jit(solution)/shard_map/ppermute | solution.py:24
  115.7 0.1 pad_maximum_fusion.5
  115.7 0.1 collective-permute-start.19
  115.9 3.3 %collective-permute-start.13 = (bf16[2,32,1536]{2,1,0:T(8,128)(2,1)S(1)}, bf16[2,32,1536]{2,1,0:T(8,128)(2,1)S(1)}, u32[]{:S(2)}, u32[]{:S(2)}) collective-permute-start(bf16[2,32,1536]{2,1,0:T(8,128)(2,1)S(1)} %pad_maximum_fusion.7), channel_id=1, source_target_pairs={{0,6},{1,7},{2,0},{3,1},{4,2},{5,3},{6,4},{7,5},{8,14},{9,15},{10,... | collective-permute-start | bytes 589832 | tf_op jit(solution)/shard_map/ppermute | solution.py:24
  119.2 0.1 collective-permute-start.14
  119.3 11.6 %collective-permute-done.18 = bf16[2,64,2560]{2,1,0:T(8,128)(2,1)S(1)} collective-permute-done((bf16[2,64,2560]{2,1,0:T(8,128)(2,1)S(1)}, bf16[2,64,2560]{2,1,0:T(8,128)(2,1)S(1)}, u32[]{:S(2)}, u32[]{:S(2)}) %collective-permute-start.18) | collective-permute-done | bytes 655392 | tf_op jit(solution)/shard_map/ppermute | solution.py:24
  130.9 3.7 %collective-permute-done.19 = bf16[2,64,2560]{2,1,0:T(8,128)(2,1)S(1)} collective-permute-done((bf16[2,64,2560]{2,1,0:T(8,128)(2,1)S(1)}, bf16[2,64,2560]{2,1,0:T(8,128)(2,1)S(1)}, u32[]{:S(2)}, u32[]{:S(2)}) %collective-permute-start.19) | collective-permute-done | bytes 655392 | tf_op jit(solution)/shard_map/ppermute | solution.py:24
  134.6 0.2 fusion.23
  134.8 0.1 collective-permute-start.20
  134.9 3.2 %collective-permute-start.21 = (bf16[64,2560]{1,0:T(8,128)(2,1)S(1)}, bf16[64,2560]{1,0:T(8,128)(2,1)S(1)}, u32[]{:S(2)}, u32[]{:S(2)}) collective-permute-start(bf16[64,2560]{1,0:T(8,128)(2,1)S(1)} %get-tuple-element.12), channel_id=1, source_target_pairs={{0,6},{1,7},{2,0},{3,1},{4,2},{5,3},{6,4},{7,5},{8,14},{9,15},{10,... | collective-permute-start | bytes 983048 | tf_op jit(solution)/shard_map/ppermute | solution.py:24
  138.1 0.7 collective-permute-done.14
  138.8 0.1 fusion.26
  138.9 0.1 collective-permute-start.15
  139.0 3.2 %collective-permute-start.16 = (bf16[32,1536]{1,0:T(8,128)(2,1)S(1)}, bf16[32,1536]{1,0:T(8,128)(2,1)S(1)}, u32[]{:S(2)}, u32[]{:S(2)}) collective-permute-start(bf16[32,1536]{1,0:T(8,128)(2,1)S(1)} %get-tuple-element.20), channel_id=1, source_target_pairs={{0,6},{1,7},{2,0},{3,1},{4,2},{5,3},{6,4},{7,5},{8,14},{9,15},{10,... | collective-permute-start | bytes 294920 | tf_op jit(solution)/shard_map/ppermute | solution.py:24
  142.2 2.6 %collective-permute-done.20 = bf16[64,2560]{1,0:T(8,128)(2,1)S(1)} collective-permute-done((bf16[64,2560]{1,0:T(8,128)(2,1)S(1)}, bf16[64,2560]{1,0:T(8,128)(2,1)S(1)}, u32[]{:S(2)}, u32[]{:S(2)}) %collective-permute-start.20) | collective-permute-done | bytes 327712 | tf_op jit(solution)/shard_map/ppermute | solution.py:24
  144.8 0.2 bitcast_add_fusion.2
  145.1 0.1 pad_maximum_fusion.1
  145.2 0.6 collective-permute-start.22
  145.9 0.0 collective-permute-done.15
  145.9 0.1 bitcast_add_fusion.4
  146.0 7.9 %collective-permute-done.22 = bf16[64,2560]{1,0:T(8,128)(2,1)S(1)} collective-permute-done((bf16[64,2560]{1,0:T(8,128)(2,1)S(1)}, bf16[64,2560]{1,0:T(8,128)(2,1)S(1)}, u32[]{:S(2)}, u32[]{:S(2)}) %collective-permute-start.22) | collective-permute-done | bytes 327712 | tf_op jit(solution)/shard_map/ppermute | solution.py:28
  153.9 0.1 bitcast_add_fusion
  153.9 1.0 pad_maximum_fusion.2
  (46 shorter events, 0.4 us)
Async XLA Ops:
  0.0 13.0 %copy-start.5 = (s32[2]{0:T(128)S(1)}, s32[2]{0:T(128)}, u32[]{:S(2)}) copy-start(s32[2]{0:T(128)} %param.10) | copy-start | bytes 28
  0.0 13.0 %copy-start.4 = (f32[4]{0:T(128)S(1)}, f32[4]{0:T(128)}, u32[]{:S(2)}) copy-start(f32[4]{0:T(128)} %param.11) | copy-start | bytes 52
  5.1 20.2 %all-to-all-start = ((bf16[16,8,16,128]{3,2,1,0:T(8,128)(2,1)}), bf16[16,8,16,128]{3,2,1,0:T(8,128)(2,1)S(1)}, u32[]{:S(2)}, u32[]{:S(2)}) async-start(bf16[16,8,16,128]{3,2,1,0:T(8,128)(2,1)} %shard_map.73), calls=%async_computation | async-start | bytes 1048576 | tf_op jit(solution)/shard_map/all_to_all | solution.py:200
  25.3 0.8 copy-start
  30.7 13.0 %copy-start.1 = (bf16[64,2048]{1,0:T(8,128)(2,1)S(1)}, bf16[64,2048]{1,0:T(8,128)(2,1)}, u32[]{:S(2)}) copy-start(bf16[64,2048]{1,0:T(8,128)(2,1)} %get-tuple-element.7) | copy-start | bytes 786436
  30.7 7.6 %collective-permute-start.6 = (bf16[64,2048]{1,0:T(8,128)(2,1)}, bf16[64,2048]{1,0:T(8,128)(2,1)S(1)}, u32[]{:S(2)}, u32[]{:S(2)}) collective-permute-start(bf16[64,2048]{1,0:T(8,128)(2,1)} %get-tuple-element.8), channel_id=1, source_target_pairs={{0,64},{16,80},{32,96},{48,112},{64,0},{80,16},{96,32},{112,48},{1... | collective-permute-start | bytes 786440 | tf_op jit(solution)/shard_map/ppermute | solution.py:40
  31.8 11.9 %collective-permute-start = (bf16[64,2048]{1,0:T(8,128)(2,1)}, bf16[64,2048]{1,0:T(8,128)(2,1)S(1)}, u32[]{:S(2)}, u32[]{:S(2)}) collective-permute-start(bf16[64,2048]{1,0:T(8,128)(2,1)} %get-tuple-element.7), channel_id=1, source_target_pairs={{0,16},{16,32},{32,48},{48,0},{64,80},{80,96},{96,112},{112,64},{1... | collective-permute-start | bytes 786440 | tf_op jit(solution)/shard_map/ppermute | solution.py:36
  33.3 10.3 %collective-permute-start.1 = (bf16[64,2048]{1,0:T(8,128)(2,1)}, bf16[64,2048]{1,0:T(8,128)(2,1)S(1)}, u32[]{:S(2)}, u32[]{:S(2)}) collective-permute-start(bf16[64,2048]{1,0:T(8,128)(2,1)} %get-tuple-element.7), channel_id=1, source_target_pairs={{0,48},{16,0},{32,16},{48,32},{64,112},{80,64},{96,80},{112,96},{1... | collective-permute-start | bytes 786440 | tf_op jit(solution)/shard_map/ppermute | solution.py:36
  39.3 14.9 %collective-permute-start.7 = (bf16[2,64,2048]{2,1,0:T(8,128)(2,1)S(1)}, bf16[2,64,2048]{2,1,0:T(8,128)(2,1)S(1)}, u32[]{:S(2)}, u32[]{:S(2)}) collective-permute-start(bf16[2,64,2048]{2,1,0:T(8,128)(2,1)S(1)} %get-tuple-element.26), channel_id=1, source_target_pairs={{0,16},{16,32},{32,48},{48,0},{64,80},{80,96},{96,112},{112,64},{1... | collective-permute-start | bytes 1572872 | tf_op jit(solution)/shard_map/ppermute | solution.py:36
  41.9 14.9 %collective-permute-start.9 = (bf16[2,64,2048]{2,1,0:T(8,128)(2,1)S(1)}, bf16[2,64,2048]{2,1,0:T(8,128)(2,1)S(1)}, u32[]{:S(2)}, u32[]{:S(2)}) collective-permute-start(bf16[2,64,2048]{2,1,0:T(8,128)(2,1)S(1)} %get-tuple-element.26), channel_id=1, source_target_pairs={{0,48},{16,0},{32,16},{48,32},{64,112},{80,64},{96,80},{112,96},{1... | collective-permute-start | bytes 1572872 | tf_op jit(solution)/shard_map/ppermute | solution.py:36
  43.6 26.6 %slice-start = ((s8[16777216]{0:T(1024)(128)(4,1)}), s8[4194304]{0:T(1024)(128)(4,1)S(1)}, s32[]{:S(2)}) async-start(s8[16777216]{0:T(1024)(128)(4,1)} %bitcast.81), calls=%async_computation.1 | async-start | bytes 8388608
  43.7 34.0 %collective-permute-start.2 = (bf16[3,64,2048]{2,1,0:T(8,128)(2,1)S(1)}, bf16[3,64,2048]{2,1,0:T(8,128)(2,1)S(1)}, u32[]{:S(2)}, u32[]{:S(2)}) collective-permute-start(bf16[3,64,2048]{2,1,0:T(8,128)(2,1)S(1)} %pad_maximum_fusion.3), channel_id=1, source_target_pairs={{0,64},{16,80},{32,96},{48,112},{64,0},{80,16},{96,32},{112,48},{1... | collective-permute-start | bytes 2359304 | tf_op jit(solution)/shard_map/ppermute | solution.py:40
  44.8 13.7 %collective-permute-start.3 = (bf16[32,2048]{1,0:T(8,128)(2,1)S(1)}, bf16[32,2048]{1,0:T(8,128)(2,1)S(1)}, u32[]{:S(2)}, u32[]{:S(2)}) collective-permute-start(bf16[32,2048]{1,0:T(8,128)(2,1)S(1)} %slice.150), channel_id=1, source_target_pairs={{0,16},{16,32},{32,48},{48,0},{64,80},{80,96},{96,112},{112,64},{1... | collective-permute-start | bytes 393224 | tf_op jit(solution)/shard_map/ppermute | solution.py:36
  45.3 14.0 %collective-permute-start.4 = (bf16[32,2048]{1,0:T(8,128)(2,1)S(1)}, bf16[32,2048]{1,0:T(8,128)(2,1)S(1)}, u32[]{:S(2)}, u32[]{:S(2)}) collective-permute-start(bf16[32,2048]{1,0:T(8,128)(2,1)S(1)} %slice.151), channel_id=1, source_target_pairs={{0,48},{16,0},{32,16},{48,32},{64,112},{80,64},{96,80},{112,96},{1... | collective-permute-start | bytes 393224 | tf_op jit(solution)/shard_map/ppermute | solution.py:36
  54.2 7.7 %collective-permute-start.8 = (bf16[64,2048]{1,0:T(8,128)(2,1)S(1)}, bf16[64,2048]{1,0:T(8,128)(2,1)S(1)}, u32[]{:S(2)}, u32[]{:S(2)}) collective-permute-start(bf16[64,2048]{1,0:T(8,128)(2,1)S(1)} %slice_bitcast_fusion.1), channel_id=1, source_target_pairs={{0,16},{16,32},{32,48},{48,0},{64,80},{80,96},{96,112},{112,64},{1... | collective-permute-start | bytes 786440 | tf_op jit(solution)/shard_map/ppermute | solution.py:36
  56.8 6.4 %collective-permute-start.10 = (bf16[64,2048]{1,0:T(8,128)(2,1)S(1)}, bf16[64,2048]{1,0:T(8,128)(2,1)S(1)}, u32[]{:S(2)}, u32[]{:S(2)}) collective-permute-start(bf16[64,2048]{1,0:T(8,128)(2,1)S(1)} %slice_bitcast_fusion), channel_id=1, source_target_pairs={{0,48},{16,0},{32,16},{48,32},{64,112},{80,64},{96,80},{112,96},{1... | collective-permute-start | bytes 786440 | tf_op jit(solution)/shard_map/ppermute | solution.py:36
  59.4 18.5 %collective-permute-start.5 = (bf16[64,2048]{1,0:T(8,128)(2,1)S(1)}, bf16[64,2048]{1,0:T(8,128)(2,1)S(1)}, u32[]{:S(2)}, u32[]{:S(2)}) collective-permute-start(bf16[64,2048]{1,0:T(8,128)(2,1)S(1)} %constant_dynamic-update-slice_fusion), channel_id=1, source_target_pairs={{0,64},{16,80},{32,96},{48,112},{64,0},{80,16},{96,32},{112,48},{1... | collective-permute-start | bytes 786440 | tf_op jit(solution)/shard_map/ppermute | solution.py:40
  63.3 7.0 %slice-start.1 = ((s8[16777216]{0:T(1024)(128)(4,1)}), s8[4194304]{0:T(1024)(128)(4,1)S(1)}, s32[]{:S(2)}) async-start(s8[16777216]{0:T(1024)(128)(4,1)} %bitcast.81), calls=%async_computation.2 | async-start | bytes 8388608
  63.5 6.7 %slice-start.2 = ((s8[16777216]{0:T(1024)(128)(4,1)}), s8[4194304]{0:T(1024)(128)(4,1)S(1)}, s32[]{:S(2)}) async-start(s8[16777216]{0:T(1024)(128)(4,1)} %bitcast.81), calls=%async_computation.3 | async-start | bytes 8388608
  63.6 6.7 %slice-start.3 = ((s8[16777216]{0:T(1024)(128)(4,1)}), s8[4194304]{0:T(1024)(128)(4,1)S(1)}, s32[]{:S(2)}) async-start(s8[16777216]{0:T(1024)(128)(4,1)} %bitcast.81), calls=%async_computation.4 | async-start | bytes 8388608
  70.0 8.0 %collective-permute-start.11 = (bf16[512,1536]{1,0:T(8,128)(2,1)S(1)}, bf16[512,1536]{1,0:T(8,128)(2,1)S(1)}, u32[]{:S(2)}, u32[]{:S(2)}) collective-permute-start(bf16[512,1536]{1,0:T(8,128)(2,1)S(1)} %fusion.19), channel_id=1, source_target_pairs={{0,1},{1,0},{2,3},{3,2},{4,5},{5,4},{6,7},{7,6},{8,9},{9,8},{10,11... | collective-permute-start | bytes 4718600 | tf_op jit(solution)/shard_map/ppermute | solution.py:32
  77.2 25.5 %collective-permute-start.17 = (bf16[512,2560]{1,0:T(8,128)(2,1)}, bf16[512,2560]{1,0:T(8,128)(2,1)}, u32[]{:S(2)}, u32[]{:S(2)}) collective-permute-start(bf16[512,2560]{1,0:T(8,128)(2,1)} %fusion.10), channel_id=1, source_target_pairs={{0,1},{1,0},{2,3},{3,2},{4,5},{5,4},{6,7},{7,6},{8,9},{9,8},{10,11... | collective-permute-start | bytes 7864328 | tf_op jit(solution)/shard_map/ppermute | solution.py:32
  77.9 3.5 %copy-start.2 = (bf16[8,64,2048]{2,1,0:T(8,128)(2,1)}, bf16[8,64,2048]{2,1,0:T(8,128)(2,1)S(1)}, u32[]{:S(2)}) copy-start(bf16[8,64,2048]{2,1,0:T(8,128)(2,1)S(1)} %slice_dynamic-update-slice_fusion) | copy-start | bytes 6291460
  81.5 21.1 %collective-permute-start.12 = (bf16[4,64,1536]{2,1,0:T(8,128)(2,1)S(1)}, bf16[4,64,1536]{2,1,0:T(8,128)(2,1)S(1)}, u32[]{:S(2)}, u32[]{:S(2)}) collective-permute-start(bf16[4,64,1536]{2,1,0:T(8,128)(2,1)S(1)} %dynamic-slice_bitcast_fusion), channel_id=1, source_target_pairs={{0,8},{1,9},{2,10},{3,11},{4,12},{5,13},{6,14},{7,15},{8,0},{9,1},... | collective-permute-start | bytes 2359304 | tf_op jit(solution)/shard_map/ppermute | solution.py:28
  83.1 19.7 %copy-start.3 = (bf16[8,64,2048]{2,1,0:T(8,128)(2,1)S(1)}, bf16[8,64,2048]{2,1,0:T(8,128)(2,1)}, u32[]{:S(2)}) copy-start(bf16[8,64,2048]{2,1,0:T(8,128)(2,1)} %copy-done.2) | copy-start | bytes 6291460
  113.2 17.7 %collective-permute-start.18 = (bf16[2,64,2560]{2,1,0:T(8,128)(2,1)S(1)}, bf16[2,64,2560]{2,1,0:T(8,128)(2,1)S(1)}, u32[]{:S(2)}, u32[]{:S(2)}) collective-permute-start(bf16[2,64,2560]{2,1,0:T(8,128)(2,1)S(1)} %pad_maximum_fusion.4), channel_id=1, source_target_pairs={{0,6},{1,7},{2,0},{3,1},{4,2},{5,3},{6,4},{7,5},{8,14},{9,15},{10,... | collective-permute-start | bytes 1966088 | tf_op jit(solution)/shard_map/ppermute | solution.py:24
  115.7 18.9 %collective-permute-start.19 = (bf16[2,64,2560]{2,1,0:T(8,128)(2,1)S(1)}, bf16[2,64,2560]{2,1,0:T(8,128)(2,1)S(1)}, u32[]{:S(2)}, u32[]{:S(2)}) collective-permute-start(bf16[2,64,2560]{2,1,0:T(8,128)(2,1)S(1)} %pad_maximum_fusion.5), channel_id=1, source_target_pairs={{0,2},{1,3},{2,4},{3,5},{4,6},{5,7},{6,0},{7,1},{8,10},{9,11},{10,... | collective-permute-start | bytes 1966088 | tf_op jit(solution)/shard_map/ppermute | solution.py:24
  115.9 22.2 %collective-permute-start.13 = (bf16[2,32,1536]{2,1,0:T(8,128)(2,1)S(1)}, bf16[2,32,1536]{2,1,0:T(8,128)(2,1)S(1)}, u32[]{:S(2)}, u32[]{:S(2)}) collective-permute-start(bf16[2,32,1536]{2,1,0:T(8,128)(2,1)S(1)} %pad_maximum_fusion.7), channel_id=1, source_target_pairs={{0,6},{1,7},{2,0},{3,1},{4,2},{5,3},{6,4},{7,5},{8,14},{9,15},{10,... | collective-permute-start | bytes 589832 | tf_op jit(solution)/shard_map/ppermute | solution.py:24
  119.2 19.6 %collective-permute-start.14 = (bf16[2,32,1536]{2,1,0:T(8,128)(2,1)S(1)}, bf16[2,32,1536]{2,1,0:T(8,128)(2,1)S(1)}, u32[]{:S(2)}, u32[]{:S(2)}) collective-permute-start(bf16[2,32,1536]{2,1,0:T(8,128)(2,1)S(1)} %pad_maximum_fusion.8), channel_id=1, source_target_pairs={{0,2},{1,3},{2,4},{3,5},{4,6},{5,7},{6,0},{7,1},{8,10},{9,11},{10,... | collective-permute-start | bytes 589832 | tf_op jit(solution)/shard_map/ppermute | solution.py:24
  134.8 10.1 %collective-permute-start.20 = (bf16[64,2560]{1,0:T(8,128)(2,1)S(1)}, bf16[64,2560]{1,0:T(8,128)(2,1)S(1)}, u32[]{:S(2)}, u32[]{:S(2)}) collective-permute-start(bf16[64,2560]{1,0:T(8,128)(2,1)S(1)} %get-tuple-element.11), channel_id=1, source_target_pairs={{0,2},{1,3},{2,4},{3,5},{4,6},{5,7},{6,0},{7,1},{8,10},{9,11},{10,... | collective-permute-start | bytes 983048 | tf_op jit(solution)/shard_map/ppermute | solution.py:24
  134.9 10.0 %collective-permute-start.21 = (bf16[64,2560]{1,0:T(8,128)(2,1)S(1)}, bf16[64,2560]{1,0:T(8,128)(2,1)S(1)}, u32[]{:S(2)}, u32[]{:S(2)}) collective-permute-start(bf16[64,2560]{1,0:T(8,128)(2,1)S(1)} %get-tuple-element.12), channel_id=1, source_target_pairs={{0,6},{1,7},{2,0},{3,1},{4,2},{5,3},{6,4},{7,5},{8,14},{9,15},{10,... | collective-permute-start | bytes 983048 | tf_op jit(solution)/shard_map/ppermute | solution.py:24
  138.9 7.0 %collective-permute-start.15 = (bf16[32,1536]{1,0:T(8,128)(2,1)S(1)}, bf16[32,1536]{1,0:T(8,128)(2,1)S(1)}, u32[]{:S(2)}, u32[]{:S(2)}) collective-permute-start(bf16[32,1536]{1,0:T(8,128)(2,1)S(1)} %get-tuple-element.19), channel_id=1, source_target_pairs={{0,2},{1,3},{2,4},{3,5},{4,6},{5,7},{6,0},{7,1},{8,10},{9,11},{10,... | collective-permute-start | bytes 294920 | tf_op jit(solution)/shard_map/ppermute | solution.py:24
  139.0 6.9 %collective-permute-start.16 = (bf16[32,1536]{1,0:T(8,128)(2,1)S(1)}, bf16[32,1536]{1,0:T(8,128)(2,1)S(1)}, u32[]{:S(2)}, u32[]{:S(2)}) collective-permute-start(bf16[32,1536]{1,0:T(8,128)(2,1)S(1)} %get-tuple-element.20), channel_id=1, source_target_pairs={{0,6},{1,7},{2,0},{3,1},{4,2},{5,3},{6,4},{7,5},{8,14},{9,15},{10,... | collective-permute-start | bytes 294920 | tf_op jit(solution)/shard_map/ppermute | solution.py:24
  145.2 8.7 %collective-permute-start.22 = (bf16[64,2560]{1,0:T(8,128)(2,1)S(1)}, bf16[64,2560]{1,0:T(8,128)(2,1)S(1)}, u32[]{:S(2)}, u32[]{:S(2)}) collective-permute-start(bf16[64,2560]{1,0:T(8,128)(2,1)S(1)} %fusion.25), channel_id=1, source_target_pairs={{0,8},{1,9},{2,10},{3,11},{4,12},{5,13},{6,14},{7,15},{8,0},{9,1},... | collective-permute-start | bytes 983048 | tf_op jit(solution)/shard_map/ppermute | solution.py:28
